TPU v7x, 32 devices: a whole 2x2x4 slice. The times are simulated.
32 devices in a mesh: gx: 2 (over core), gy: 4 (over y, x), gz: 4 (over z).
Axes of the slice: x: 2, y: 2, z: 4, core: 2. Of those that a mesh axis runs over, the one named last changes fastest.
Arguments:
- flexibility: bfloat16 [4, 4, 4, 1536, 1536], P('gx', 'gy', 'gz'), may hold values from -3 to 3, as said below
- dual_load: float32 [4, 4, 4, 3, 256, 128], P('gx', 'gy', 'gz'), may hold values from -20 to 20
- coarse_load: float32 [4, 4, 4, 128], replicated, may hold values from -384 to 384
- glue: int32 [4, 4, 4, 3], replicated, may hold values 0 or 1
- floating_flag: int32 [4, 4, 4], replicated, may hold values 0 or 1
Outputs:
- multipliers: float32 [4, 4, 4, 3, 256, 128], P('gx', 'gy', 'gz')
- residual: float32 [4, 4, 4, 3, 256, 128], P('gx', 'gy', 'gz')
Inputs may be any that keep to these rules, and one draw needn't show every extreme that they name: `flexibility`: for every subdomain the [1536, 1536] matrix is symmetric and positive definite.
All inputs are finite; a program needn't handle non-finite values.
Results may differ from a plain program's by a relative error of at most 0.015.
Values sent between devices are 32-bit elements; how exact they have to be, the bound alone decides.
A program may use at most 128 MiB of HBM per device.

v0:
```python
import math

import jax
import jax.numpy as jnp
from jax import lax
from jax.sharding import PartitionSpec as P

ITERS = 4


def padded_2(cells, sides, width):
    for axis, dim in sides:
        count = lax.axis_size(axis)
        ends = count - 1
        head = lax.slice_in_dim(cells, 0, width, axis=dim)
        tail = lax.slice_in_dim(cells, cells.shape[dim] - width, cells.shape[dim], axis=dim)
        cells = jnp.concatenate(
            [
                lax.ppermute(tail, axis, [(i, (i + 1) % count) for i in range(ends)]),
                cells,
                lax.ppermute(head, axis, [((i + 1) % count, i) for i in range(ends)]),
            ],
            axis=dim,
        )
    return cells


def shifted(values, dimension, toward):
    length = values.shape[dimension]
    widths = [(0, 0)] * values.ndim
    if toward > 0:
        widths[dimension] = (0, 1)
        return lax.slice_in_dim(jnp.pad(values, widths), 1, length + 1, axis=dimension)
    widths[dimension] = (1, 0)
    return lax.slice_in_dim(jnp.pad(values, widths), 0, length, axis=dimension)


def coupling(glue, floating_flag):
    grid_shape = floating_flag.shape
    active = []
    for dimension in range(3):
        coordinate = lax.broadcasted_iota(jnp.int32, grid_shape, dimension)
        inside = (coordinate < grid_shape[dimension] - 1).astype(jnp.int32)
        active.append(inside * glue[..., dimension])
    return (jnp.stack(active, axis=-1), floating_flag)


def coarse_matrix(active, floating):
    grid_shape = floating.shape
    total_count = grid_shape[0] * grid_shape[1] * grid_shape[2]
    strides = (grid_shape[1] * grid_shape[2], grid_shape[2], 1)
    support = 2.0 / float(grid_shape[0] * grid_shape[0])
    degree = jnp.zeros(grid_shape, jnp.int32)
    for dimension in range(3):
        degree = degree + active[..., dimension] + shifted(active[..., dimension], dimension, -1)
    flat_float = floating.reshape(total_count).astype(jnp.float32)
    diagonal = jnp.where(
        flat_float > 0, degree.reshape(total_count).astype(jnp.float32) + support, 1.0
    )
    row_index = lax.broadcasted_iota(jnp.int32, (total_count, total_count), 0)
    col_index = lax.broadcasted_iota(jnp.int32, (total_count, total_count), 1)
    matrix = jnp.where(row_index == col_index, diagonal[:, None], 0.0)
    for dimension in range(3):
        link_weight = (
            (active[..., dimension] * floating * shifted(floating, dimension, 1))
            .reshape(total_count)
            .astype(jnp.float32)
        )
        upper_band = jnp.where(
            col_index == row_index + strides[dimension], link_weight[:, None], 0.0
        )
        matrix = matrix - upper_band - upper_band.T
    return matrix


def alternate(low_part, high_part, dimension):
    joined = jnp.stack([low_part, high_part], axis=dimension + 1)
    new_shape = (
        low_part.shape[:dimension]
        + (2 * low_part.shape[dimension],)
        + low_part.shape[dimension + 1 :]
    )
    return joined.reshape(new_shape)


def separate(padded, dimension, layers):
    from_above = lax.slice_in_dim(padded, 3, 2 * layers + 2, stride=2, axis=dimension)
    from_below = lax.slice_in_dim(padded, 0, 2 * layers, stride=2, axis=dimension)
    return (from_above, from_below)


def per_device(flexibility, dual_load, coarse_load, glue, floating_flag):
    block_x, block_y, block_z = (dual_load.shape[0], dual_load.shape[1], dual_load.shape[2])
    face_dofs, cases = (dual_load.shape[4], dual_load.shape[5])
    grid_x, grid_y, grid_z = floating_flag.shape
    subdomains = grid_x * grid_y * grid_z
    local_count = block_x * block_y * block_z
    start_x = lax.axis_index("gx") * block_x
    start_y = lax.axis_index("gy") * block_y
    start_z = lax.axis_index("gz") * block_z
    active_int, floating_int = coupling(glue, floating_flag)
    factor = jnp.linalg.cholesky(coarse_matrix(active_int, floating_int))
    mode_value = 1.0 / math.sqrt(face_dofs)
    support_value = 2.0 / float(grid_x * grid_x)
    active_global = active_int.astype(jnp.float32)
    below_global = jnp.stack(
        [shifted(active_global[..., dimension], dimension, -1) for dimension in range(3)], axis=-1
    )
    floating_global = floating_int.astype(jnp.float32)
    full_shape = (block_x, block_y, block_z, 3, face_dofs, cases)

    def own_block(values):
        return lax.dynamic_slice(
            values,
            (start_x, start_y, start_z) + (0,) * (values.ndim - 3),
            (block_x, block_y, block_z) + values.shape[3:],
        )

    upper_active = own_block(active_global)
    lower_active = own_block(below_global)
    upper_mask = upper_active[..., None, None]
    lower_mask = lower_active[..., None, None]
    floating_block = own_block(floating_global)
    matrices = flexibility.reshape(local_count, 6 * face_dofs, 6 * face_dofs)

    def operate(upper_part, lower_part, offset):
        face_list = []
        for dimension in range(3):
            face_list.append(-lower_part[:, :, :, dimension])
            face_list.append(upper_part[:, :, :, dimension])
        face_loads = (
            jnp.stack(face_list, axis=3)
            .astype(jnp.bfloat16)
            .reshape(local_count, 6 * face_dofs, cases)
        )
        traces = jnp.einsum(
            "sij,sjr->sir", matrices, face_loads, preferred_element_type=jnp.float32
        )
        traces = traces.reshape(block_x, block_y, block_z, 6, face_dofs, cases)
        low_face = traces[:, :, :, 0::2]
        high_face = traces[:, :, :, 1::2] - offset
        padded_x = padded_2(
            alternate(low_face[:, :, :, 0], high_face[:, :, :, 0], 0), (("gx", 0),), 1
        )
        above_x, below_x = separate(padded_x, 0, block_x)
        padded_y = padded_2(
            alternate(low_face[:, :, :, 1], high_face[:, :, :, 1], 1), (("gy", 1),), 1
        )
        above_y, below_y = separate(padded_y, 1, block_y)
        padded_z = padded_2(
            alternate(low_face[:, :, :, 2], high_face[:, :, :, 2], 2), (("gz", 2),), 1
        )
        above_z, below_z = separate(padded_z, 2, block_z)
        upper_jump = upper_mask * (high_face - jnp.stack([above_x, above_y, above_z], axis=3))
        lower_jump = lower_mask * (jnp.stack([below_x, below_y, below_z], axis=3) - low_face)
        return (upper_jump, lower_jump)

    def coarse_solve(source):
        return jax.scipy.linalg.cho_solve(
            (factor, True), source.reshape(subdomains, cases)
        ).reshape(grid_x, grid_y, grid_z, cases)

    def correction(amplitude):
        padded = jnp.pad(amplitude, ((1, 1), (1, 1), (1, 1), (0, 0)))
        window = lax.dynamic_slice(
            padded, (start_x, start_y, start_z, 0), (block_x + 2, block_y + 2, block_z + 2, cases)
        )
        centre = window[1:-1, 1:-1, 1:-1]
        upward = [window[2:, 1:-1, 1:-1], window[1:-1, 2:, 1:-1], window[1:-1, 1:-1, 2:]]
        downward = [window[:-2, 1:-1, 1:-1], window[1:-1, :-2, 1:-1], window[1:-1, 1:-1, :-2]]
        upper_part = jnp.stack(
            [
                upper_active[..., dimension, None] * mode_value * (centre - upward[dimension])
                for dimension in range(3)
            ],
            axis=3,
        )
        lower_part = jnp.stack(
            [
                lower_active[..., dimension, None] * mode_value * (downward[dimension] - centre)
                for dimension in range(3)
            ],
            axis=3,
        )
        return (upper_part[:, :, :, :, None, :], lower_part[:, :, :, :, None, :])

    def assemble(block):
        canvas = jnp.zeros((grid_x, grid_y, grid_z, cases), jnp.float32)
        canvas = lax.dynamic_update_slice(canvas, block, (start_x, start_y, start_z, 0))
        arranged = lax.psum(canvas, ("gx", "gy", "gz"))
        return arranged

    def coarse_source(upper_part, lower_part):
        return (
            mode_value * floating_block[..., None] * jnp.sum(upper_part - lower_part, axis=(3, 4))
        )

    def inner_sums(left, right):
        return jnp.sum(left * right, axis=(0, 1, 2, 3, 4))

    def projected_norm(squared_value, source_value, amplitude_value):
        removed = jnp.sum(source_value * amplitude_value, axis=(0, 1, 2))
        removed = removed + support_value * jnp.sum(
            amplitude_value * amplitude_value, axis=(0, 1, 2)
        )
        return squared_value - removed

    def totals(stacked):
        return lax.psum(stacked, ("gx", "gy", "gz"))

    start_amplitude = coarse_solve(floating_global[..., None] * coarse_load)
    spread_upper, spread_lower = correction(start_amplitude)
    multiplier_upper = jnp.broadcast_to(spread_upper, full_shape)
    multiplier_lower = jnp.broadcast_to(spread_lower, full_shape)
    jump_upper, jump_lower = operate(multiplier_upper, multiplier_lower, dual_load)
    residual_upper = -jump_upper
    residual_lower = -jump_lower
    source = assemble(coarse_source(residual_upper, residual_lower))
    squared = totals(inner_sums(residual_upper, residual_upper)[None])[0]
    amplitude = coarse_solve(source)
    spread_upper, spread_lower = correction(amplitude)
    projected_upper = residual_upper - spread_upper
    projected_lower = residual_lower - spread_lower
    current = projected_norm(squared, source, amplitude)
    search_upper, search_lower = (projected_upper, projected_lower)
    for iteration in range(ITERS):
        applied_upper, applied_lower = operate(search_upper, search_lower, 0.0)
        partial_sums = totals(
            jnp.stack(
                [
                    inner_sums(search_upper, applied_upper),
                    inner_sums(residual_upper, applied_upper),
                    inner_sums(applied_upper, applied_upper),
                ]
            )
        )
        curvature = partial_sums[0]
        step_size = current / curvature
        multiplier_upper = multiplier_upper + step_size * search_upper
        multiplier_lower = multiplier_lower + step_size * search_lower
        residual_upper = residual_upper - step_size * applied_upper
        residual_lower = residual_lower - step_size * applied_lower
        source = assemble(coarse_source(residual_upper, residual_lower))
        amplitude = coarse_solve(source)
        spread_upper, spread_lower = correction(amplitude)
        projected_upper = residual_upper - spread_upper
        projected_lower = residual_lower - spread_lower
        squared = (
            squared - 2.0 * step_size * partial_sums[1] + step_size * step_size * partial_sums[2]
        )
        renewed = projected_norm(squared, source, amplitude)
        if iteration + 1 < ITERS:
            ratio = renewed / current
            search_upper = projected_upper + ratio * search_upper
            search_lower = projected_lower + ratio * search_lower
            current = renewed
    return (multiplier_upper, projected_upper)


def solution(mesh):
    return jax.shard_map(
        per_device,
        mesh=mesh,
        in_specs=(
            P("gx", "gy", "gz", None, None),
            P("gx", "gy", "gz", None, None, None),
            P(),
            P(),
            P(),
        ),
        out_specs=(P("gx", "gy", "gz", None, None, None), P("gx", "gy", "gz", None, None, None)),
        check_vma=False,
    )
```

profile of v0, /device:TPU:0, one launch (start us, length us, event | category | flops | bytes accessed | tf_op | source)
XLA Modules:
  0.0 567.9 jit_solution(11340886455706647938)
XLA Ops:
  3.8 5.8 %cholesky.19 = f32[64,64]{1,0:T(8,128)S(1)} custom-call(f32[64,64]{1,0:T(8,128)S(1)} %fusion.69), custom_call_target="Cholesky" | custom-call | tf_op jit(solution)/shard_map/jit(cholesky)/cholesky | solution.py:102
  18.1 6.9 %fusion.10 = f32[2,1536,128]{1,2,0:T(8,128)S(1)} fusion(bf16[2,1536,128]{2,1,0:T(8,128)(2,1)S(1)} %bitcast.457, bf16[2,1,1,1536,1536]{4,3,2,1,0:T(8,128)(2,1)} %param.7), kind=kOutput, calls=%fused_computation.10 | convolution fusion | flops 1207959552 | bytes 11796480 | tf_op jit(solution)/shard_map/sij,sjr->sir/dot_general | solution.py:136
  34.9 5.5 collective-permute-start.4
  56.1 41.0 %psum.71 = f32[4,4,4,128]{3,2,1,0:T(4,128)S(1)} all-reduce(f32[4,4,4,128]{3,2,1,0:T(4,128)S(1)} %dynamic_update_slice.15), channel_id=1, replica_groups=mesh['gx'=2,'gy'=4,'gz'=4] {'gx','gy','gz'}, use_global_device_ids=true, to_apply=%region_5.7 | all-reduce | flops 8192 | bytes 65536 | tf_op jit(solution)/shard_map/psum | solution.py:190
  98.6 6.9 %fusion.13 = f32[2,1536,128]{1,2,0:T(8,128)S(1)} fusion(bf16[2,1536,128]{2,1,0:T(8,128)(2,1)S(1)} %bitcast.458, bf16[2,1,1,1536,1536]{4,3,2,1,0:T(8,128)(2,1)} %param.7), kind=kOutput, calls=%fused_computation.11 | convolution fusion | flops 1207959552 | bytes 11796480 | tf_op jit(solution)/shard_map/sij,sjr->sir/dot_general | solution.py:136
  115.6 5.5 collective-permute-start.10
  121.7 5.3 collective-permute-start.11
  127.5 40.5 %all-reduce.15 = (f32[3,128]{1,0:T(4,128)S(1)}, f32[128]{0:T(128)S(1)}) all-reduce(f32[3,128]{1,0:T(4,128)S(1)} %pad_maximum_fusion.14, f32[128]{0:T(128)S(1)} %get-tuple-element.19), channel_id=1, replica_groups=mesh['gx'=2,'gy'=4,'gz'=4] {'gx','gy','gz'}, use_global_device_ids=true, to_apply=%region_11.13 | all-reduce | flops 512 | bytes 4096 | tf_op jit(solution)/shard_map/psum | solution.py:209
  170.9 39.8 %psum.73 = f32[4,4,4,128]{3,2,1,0:T(4,128)S(1)} all-reduce(f32[4,4,4,128]{3,2,1,0:T(4,128)S(1)} %dynamic_update_slice.16), channel_id=1, replica_groups=mesh['gx'=2,'gy'=4,'gz'=4] {'gx','gy','gz'}, use_global_device_ids=true, to_apply=%region_13.15 | all-reduce | flops 8192 | bytes 65536 | tf_op jit(solution)/shard_map/psum | solution.py:190
  214.0 8.1 %fusion.16 = f32[2,1536,128]{1,2,0:T(8,128)} fusion(bf16[2,1536,128]{2,1,0:T(8,128)(2,1)S(1)} %bitcast.460, bf16[2,1,1,1536,1536]{4,3,2,1,0:T(8,128)(2,1)} %param.7), kind=kOutput, calls=%fused_computation.12 | convolution fusion | flops 1207959552 | bytes 11796480 | tf_op jit(solution)/shard_map/sij,sjr->sir/dot_general | solution.py:136
  232.3 5.5 collective-permute-start.16
  237.8 5.3 collective-permute-start.17
  244.4 41.1 %psum.74 = f32[3,128]{1,0:T(4,128)S(1)} all-reduce(f32[3,128]{1,0:T(4,128)S(1)} %pad_maximum_fusion.15), channel_id=1, replica_groups=mesh['gx'=2,'gy'=4,'gz'=4] {'gx','gy','gz'}, use_global_device_ids=true, to_apply=%region_19.21 | all-reduce | flops 384 | bytes 3072 | tf_op jit(solution)/shard_map/psum | solution.py:209
  288.5 40.0 %psum.75 = f32[4,4,4,128]{3,2,1,0:T(4,128)S(1)} all-reduce(f32[4,4,4,128]{3,2,1,0:T(4,128)S(1)} %dynamic_update_slice.17), channel_id=1, replica_groups=mesh['gx'=2,'gy'=4,'gz'=4] {'gx','gy','gz'}, use_global_device_ids=true, to_apply=%region_21.23 | all-reduce | flops 8192 | bytes 65536 | tf_op jit(solution)/shard_map/psum | solution.py:190
  331.8 8.0 %fusion.19 = f32[2,1536,128]{1,2,0:T(8,128)} fusion(bf16[2,1536,128]{2,1,0:T(8,128)(2,1)S(1)} %bitcast.461, bf16[2,1,1,1536,1536]{4,3,2,1,0:T(8,128)(2,1)} %param.7), kind=kOutput, calls=%fused_computation.13 | convolution fusion | flops 1207959552 | bytes 11796480 | tf_op jit(solution)/shard_map/sij,sjr->sir/dot_general | solution.py:136
  351.4 5.5 collective-permute-start.22
  356.9 5.2 collective-permute-start.23
  363.7 40.4 %psum.76 = f32[3,128]{1,0:T(4,128)S(1)} all-reduce(f32[3,128]{1,0:T(4,128)S(1)} %pad_maximum_fusion.16), channel_id=1, replica_groups=mesh['gx'=2,'gy'=4,'gz'=4] {'gx','gy','gz'}, use_global_device_ids=true, to_apply=%region_27.29 | all-reduce | flops 384 | bytes 3072 | tf_op jit(solution)/shard_map/psum | solution.py:209
  407.5 39.8 %psum.77 = f32[4,4,4,128]{3,2,1,0:T(4,128)S(1)} all-reduce(f32[4,4,4,128]{3,2,1,0:T(4,128)S(1)} %dynamic_update_slice.18), channel_id=1, replica_groups=mesh['gx'=2,'gy'=4,'gz'=4] {'gx','gy','gz'}, use_global_device_ids=true, to_apply=%region_29.31 | all-reduce | flops 8192 | bytes 65536 | tf_op jit(solution)/shard_map/psum | solution.py:190
  449.8 8.1 %fusion.22 = f32[2,1536,128]{1,2,0:T(8,128)} fusion(bf16[2,1536,128]{2,1,0:T(8,128)(2,1)S(1)} %bitcast.459, bf16[2,1,1,1536,1536]{4,3,2,1,0:T(8,128)(2,1)} %param.7), kind=kOutput, calls=%fused_computation.14 | convolution fusion | flops 1207959552 | bytes 11796480 | tf_op jit(solution)/shard_map/sij,sjr->sir/dot_general | solution.py:136
  469.3 5.5 collective-permute-start.28
  474.8 5.2 collective-permute-start.29
  481.7 40.6 %psum.78 = f32[3,128]{1,0:T(4,128)S(1)} all-reduce(f32[3,128]{1,0:T(4,128)S(1)} %pad_maximum_fusion.17), channel_id=1, replica_groups=mesh['gx'=2,'gy'=4,'gz'=4] {'gx','gy','gz'}, use_global_device_ids=true, to_apply=%region_35.37 | all-reduce | flops 384 | bytes 3072 | tf_op jit(solution)/shard_map/psum | solution.py:209
  524.6 39.8 %psum.79 = f32[64,128]{1,0:T(8,128)S(1)} all-reduce(f32[64,128]{1,0:T(8,128)S(1)} %bitcast.490), channel_id=1, replica_groups=mesh['gx'=2,'gy'=4,'gz'=4] {'gx','gy','gz'}, use_global_device_ids=true, to_apply=%region_37.39 | all-reduce | flops 8192 | bytes 65536 | tf_op jit(solution)/shard_map/psum | solution.py:190
  (318 shorter events, 110.6 us)
Async XLA Ops:
  28.4 14.6 %collective-permute-start = (f32[1,1,1,256,128]{4,3,0,2,1:T(8,128)}, f32[1,1,1,256,128]{4,3,0,2,1:T(8,128)}, u32[]{:S(2)}, u32[]{:S(2)}) collective-permute-start(f32[1,1,1,256,128]{4,3,0,2,1:T(8,128)} %get-tuple-element.151), channel_id=1, source_target_pairs={{0,16},{1,17},{2,18},{3,19},{4,20},{5,21},{6,22},{7,23},{8,24},{9,... | collective-permute-start | bytes 393224 | tf_op jit(solution)/shard_map/ppermute | solution.py:19
  31.4 16.2 %collective-permute-start.1 = (f32[1,1,1,256,128]{4,3,0,2,1:T(8,128)}, f32[1,1,1,256,128]{4,3,0,2,1:T(8,128)}, u32[]{:S(2)}, u32[]{:S(2)}) collective-permute-start(f32[1,1,1,256,128]{4,3,0,2,1:T(8,128)} %get-tuple-element.152), channel_id=1, source_target_pairs={{16,0},{17,1},{18,2},{19,3},{20,4},{21,5},{22,6},{23,7},{24,8},{25... | collective-permute-start | bytes 393224 | tf_op jit(solution)/shard_map/ppermute | solution.py:21
  33.6 15.1 %collective-permute-start.2 = (f32[2,1,1,256,128]{4,3,0,2,1:T(8,128)}, f32[2,1,1,256,128]{4,3,0,2,1:T(8,128)S(1)}, u32[]{:S(2)}, u32[]{:S(2)}) collective-permute-start(f32[2,1,1,256,128]{4,3,0,2,1:T(8,128)} %get-tuple-element.148), channel_id=1, source_target_pairs={{4,0},{8,4},{12,8},{5,1},{9,5},{13,9},{6,2},{10,6},{14,10},{7,3},{... | collective-permute-start | bytes 786440 | tf_op jit(solution)/shard_map/ppermute | solution.py:21
  34.9 13.8 %collective-permute-start.4 = (f32[2,1,1,256,128]{4,3,0,2,1:T(8,128)}, f32[2,1,1,256,128]{4,3,0,2,1:T(8,128)}, u32[]{:S(2)}, u32[]{:S(2)}) collective-permute-start(f32[2,1,1,256,128]{4,3,0,2,1:T(8,128)} %get-tuple-element.147), channel_id=1, source_target_pairs={{0,4},{4,8},{8,12},{1,5},{5,9},{9,13},{2,6},{6,10},{10,14},{3,7},{... | collective-permute-start | bytes 786440 | tf_op jit(solution)/shard_map/ppermute | solution.py:19
  108.9 12.8 %collective-permute-start.6 = (f32[1,1,1,256,128]{4,3,0,2,1:T(8,128)S(1)}, f32[1,1,1,256,128]{4,3,0,2,1:T(8,128)S(1)}, u32[]{:S(2)}, u32[]{:S(2)}) collective-permute-start(f32[1,1,1,256,128]{4,3,0,2,1:T(8,128)S(1)} %get-tuple-element.145), channel_id=1, source_target_pairs={{0,16},{1,17},{2,18},{3,19},{4,20},{5,21},{6,22},{7,23},{8,24},{9,... | collective-permute-start | bytes 393224 | tf_op jit(solution)/shard_map/ppermute | solution.py:19
  110.2 16.8 %collective-permute-start.7 = (f32[1,1,1,256,128]{4,3,0,2,1:T(8,128)S(1)}, f32[1,1,1,256,128]{4,3,0,2,1:T(8,128)S(1)}, u32[]{:S(2)}, u32[]{:S(2)}) collective-permute-start(f32[1,1,1,256,128]{4,3,0,2,1:T(8,128)S(1)} %get-tuple-element.146), channel_id=1, source_target_pairs={{16,0},{17,1},{18,2},{19,3},{20,4},{21,5},{22,6},{23,7},{24,8},{25... | collective-permute-start | bytes 393224 | tf_op jit(solution)/shard_map/ppermute | solution.py:21
  112.3 14.8 %collective-permute-start.8 = (f32[2,1,1,256,128]{4,3,0,2,1:T(8,128)S(1)}, f32[2,1,1,256,128]{4,3,0,2,1:T(8,128)S(1)}, u32[]{:S(2)}, u32[]{:S(2)}) collective-permute-start(f32[2,1,1,256,128]{4,3,0,2,1:T(8,128)S(1)} %get-tuple-element.142), channel_id=1, source_target_pairs={{4,0},{8,4},{12,8},{5,1},{9,5},{13,9},{6,2},{10,6},{14,10},{7,3},{... | collective-permute-start | bytes 786440 | tf_op jit(solution)/shard_map/ppermute | solution.py:21
  114.3 12.8 %collective-permute-start.9 = (f32[2,1,1,256,128]{4,3,0,2,1:T(8,128)S(1)}, f32[2,1,1,256,128]{4,3,0,2,1:T(8,128)S(1)}, u32[]{:S(2)}, u32[]{:S(2)}) collective-permute-start(f32[2,1,1,256,128]{4,3,0,2,1:T(8,128)S(1)} %get-tuple-element.144), channel_id=1, source_target_pairs={{1,0},{2,1},{3,2},{5,4},{6,5},{7,6},{9,8},{10,9},{11,10},{13,12},{... | collective-permute-start | bytes 786440 | tf_op jit(solution)/shard_map/ppermute | solution.py:21
  115.6 52.4 %collective-permute-start.10 = (f32[2,1,1,256,128]{4,3,0,2,1:T(8,128)}, f32[2,1,1,256,128]{4,3,0,2,1:T(8,128)}, u32[]{:S(2)}, u32[]{:S(2)}) collective-permute-start(f32[2,1,1,256,128]{4,3,0,2,1:T(8,128)} %get-tuple-element.141), channel_id=1, source_target_pairs={{0,4},{4,8},{8,12},{1,5},{5,9},{9,13},{2,6},{6,10},{10,14},{3,7},{... | collective-permute-start | bytes 786440 | tf_op jit(solution)/shard_map/ppermute | solution.py:19
  121.7 46.3 %collective-permute-start.11 = (f32[2,1,1,256,128]{4,3,2,0,1:T(8,128)}, f32[2,1,1,256,128]{4,3,2,0,1:T(8,128)}, u32[]{:S(2)}, u32[]{:S(2)}) collective-permute-start(f32[2,1,1,256,128]{4,3,2,0,1:T(8,128)} %get-tuple-element.143), channel_id=1, source_target_pairs={{0,1},{1,2},{2,3},{4,5},{5,6},{6,7},{8,9},{9,10},{10,11},{12,13},{... | collective-permute-start | bytes 786440 | tf_op jit(solution)/shard_map/ppermute | solution.py:19
  227.4 15.7 %collective-permute-start.13 = (f32[1,1,1,256,128]{4,3,0,2,1:T(8,128)S(1)}, f32[1,1,1,256,128]{4,3,0,2,1:T(8,128)S(1)}, u32[]{:S(2)}, u32[]{:S(2)}) collective-permute-start(f32[1,1,1,256,128]{4,3,0,2,1:T(8,128)S(1)} %get-tuple-element.140), channel_id=1, source_target_pairs={{16,0},{17,1},{18,2},{19,3},{20,4},{21,5},{22,6},{23,7},{24,8},{25... | collective-permute-start | bytes 393224 | tf_op jit(solution)/shard_map/ppermute | solution.py:21
  229.5 13.7 %collective-permute-start.14 = (f32[2,1,1,256,128]{4,3,0,1,2:T(8,128)S(1)}, f32[2,1,1,256,128]{4,3,0,1,2:T(8,128)S(1)}, u32[]{:S(2)}, u32[]{:S(2)}) collective-permute-start(f32[2,1,1,256,128]{4,3,0,1,2:T(8,128)S(1)} %get-tuple-element.135), channel_id=1, source_target_pairs={{4,0},{8,4},{12,8},{5,1},{9,5},{13,9},{6,2},{10,6},{14,10},{7,3},{... | collective-permute-start | bytes 786440 | tf_op jit(solution)/shard_map/ppermute | solution.py:21
  232.3 53.2 %collective-permute-start.16 = (f32[2,1,1,256,128]{4,3,0,1,2:T(8,128)}, f32[2,1,1,256,128]{4,3,0,1,2:T(8,128)}, u32[]{:S(2)}, u32[]{:S(2)}) collective-permute-start(f32[2,1,1,256,128]{4,3,0,1,2:T(8,128)} %get-tuple-element.136), channel_id=1, source_target_pairs={{0,4},{4,8},{8,12},{1,5},{5,9},{9,13},{2,6},{6,10},{10,14},{3,7},{... | collective-permute-start | bytes 786440 | tf_op jit(solution)/shard_map/ppermute | solution.py:19
  237.8 47.7 %collective-permute-start.17 = (f32[2,1,1,256,128]{4,3,0,2,1:T(8,128)S(1)}, f32[2,1,1,256,128]{4,3,0,2,1:T(8,128)}, u32[]{:S(2)}, u32[]{:S(2)}) collective-permute-start(f32[2,1,1,256,128]{4,3,0,2,1:T(8,128)S(1)} %get-tuple-element.138), channel_id=1, source_target_pairs={{0,1},{1,2},{2,3},{4,5},{5,6},{6,7},{8,9},{9,10},{10,11},{12,13},{... | collective-permute-start | bytes 786440 | tf_op jit(solution)/shard_map/ppermute | solution.py:19
  345.9 16.2 %collective-permute-start.19 = (f32[1,1,1,256,128]{4,3,0,2,1:T(8,128)S(1)}, f32[1,1,1,256,128]{4,3,0,2,1:T(8,128)S(1)}, u32[]{:S(2)}, u32[]{:S(2)}) collective-permute-start(f32[1,1,1,256,128]{4,3,0,2,1:T(8,128)S(1)} %get-tuple-element.134), channel_id=1, source_target_pairs={{16,0},{17,1},{18,2},{19,3},{20,4},{21,5},{22,6},{23,7},{24,8},{25... | collective-permute-start | bytes 393224 | tf_op jit(solution)/shard_map/ppermute | solution.py:21
  348.0 14.9 %collective-permute-start.20 = (f32[2,1,1,256,128]{4,3,0,2,1:T(8,128)S(1)}, f32[2,1,1,256,128]{4,3,0,2,1:T(8,128)S(1)}, u32[]{:S(2)}, u32[]{:S(2)}) collective-permute-start(f32[2,1,1,256,128]{4,3,0,2,1:T(8,128)S(1)} %get-tuple-element.129), channel_id=1, source_target_pairs={{4,0},{8,4},{12,8},{5,1},{9,5},{13,9},{6,2},{10,6},{14,10},{7,3},{... | collective-permute-start | bytes 786440 | tf_op jit(solution)/shard_map/ppermute | solution.py:21
  350.1 12.9 %collective-permute-start.21 = (f32[2,1,1,256,128]{4,3,0,2,1:T(8,128)S(1)}, f32[2,1,1,256,128]{4,3,0,2,1:T(8,128)S(1)}, u32[]{:S(2)}, u32[]{:S(2)}) collective-permute-start(f32[2,1,1,256,128]{4,3,0,2,1:T(8,128)S(1)} %get-tuple-element.131), channel_id=1, source_target_pairs={{1,0},{2,1},{3,2},{5,4},{6,5},{7,6},{9,8},{10,9},{11,10},{13,12},{... | collective-permute-start | bytes 786440 | tf_op jit(solution)/shard_map/ppermute | solution.py:21
  351.4 52.8 %collective-permute-start.22 = (f32[2,1,1,256,128]{4,3,0,2,1:T(8,128)}, f32[2,1,1,256,128]{4,3,0,2,1:T(8,128)}, u32[]{:S(2)}, u32[]{:S(2)}) collective-permute-start(f32[2,1,1,256,128]{4,3,0,2,1:T(8,128)} %get-tuple-element.130), channel_id=1, source_target_pairs={{0,4},{4,8},{8,12},{1,5},{5,9},{9,13},{2,6},{6,10},{10,14},{3,7},{... | collective-permute-start | bytes 786440 | tf_op jit(solution)/shard_map/ppermute | solution.py:19
  356.9 47.3 %collective-permute-start.23 = (f32[2,1,1,256,128]{4,3,2,0,1:T(8,128)}, f32[2,1,1,256,128]{4,3,2,0,1:T(8,128)}, u32[]{:S(2)}, u32[]{:S(2)}) collective-permute-start(f32[2,1,1,256,128]{4,3,2,0,1:T(8,128)} %get-tuple-element.132), channel_id=1, source_target_pairs={{0,1},{1,2},{2,3},{4,5},{5,6},{6,7},{8,9},{9,10},{10,11},{12,13},{... | collective-permute-start | bytes 786440 | tf_op jit(solution)/shard_map/ppermute | solution.py:19
  463.9 16.2 %collective-permute-start.25 = (f32[1,1,1,256,128]{4,3,0,2,1:T(8,128)S(1)}, f32[1,1,1,256,128]{4,3,0,2,1:T(8,128)S(1)}, u32[]{:S(2)}, u32[]{:S(2)}) collective-permute-start(f32[1,1,1,256,128]{4,3,0,2,1:T(8,128)S(1)} %get-tuple-element.128), channel_id=1, source_target_pairs={{16,0},{17,1},{18,2},{19,3},{20,4},{21,5},{22,6},{23,7},{24,8},{25... | collective-permute-start | bytes 393224 | tf_op jit(solution)/shard_map/ppermute | solution.py:21
  466.0 14.9 %collective-permute-start.26 = (f32[2,1,1,256,128]{4,3,0,2,1:T(8,128)S(1)}, f32[2,1,1,256,128]{4,3,0,2,1:T(8,128)S(1)}, u32[]{:S(2)}, u32[]{:S(2)}) collective-permute-start(f32[2,1,1,256,128]{4,3,0,2,1:T(8,128)S(1)} %get-tuple-element.124), channel_id=1, source_target_pairs={{4,0},{8,4},{12,8},{5,1},{9,5},{13,9},{6,2},{10,6},{14,10},{7,3},{... | collective-permute-start | bytes 786440 | tf_op jit(solution)/shard_map/ppermute | solution.py:21
  468.0 12.9 %collective-permute-start.27 = (f32[2,1,1,256,128]{4,3,0,2,1:T(8,128)S(1)}, f32[2,1,1,256,128]{4,3,0,2,1:T(8,128)S(1)}, u32[]{:S(2)}, u32[]{:S(2)}) collective-permute-start(f32[2,1,1,256,128]{4,3,0,2,1:T(8,128)S(1)} %get-tuple-element.126), channel_id=1, source_target_pairs={{1,0},{2,1},{3,2},{5,4},{6,5},{7,6},{9,8},{10,9},{11,10},{13,12},{... | collective-permute-start | bytes 786440 | tf_op jit(solution)/shard_map/ppermute | solution.py:21
  469.3 53.0 %collective-permute-start.28 = (f32[2,1,1,256,128]{4,3,0,2,1:T(8,128)}, f32[2,1,1,256,128]{4,3,0,2,1:T(8,128)}, u32[]{:S(2)}, u32[]{:S(2)}) collective-permute-start(f32[2,1,1,256,128]{4,3,0,2,1:T(8,128)} %get-tuple-element.123), channel_id=1, source_target_pairs={{0,4},{4,8},{8,12},{1,5},{5,9},{9,13},{2,6},{6,10},{10,14},{3,7},{... | collective-permute-start | bytes 786440 | tf_op jit(solution)/shard_map/ppermute | solution.py:19
  474.8 47.5 %collective-permute-start.29 = (f32[2,1,1,256,128]{4,3,2,0,1:T(8,128)}, f32[2,1,1,256,128]{4,3,2,0,1:T(8,128)}, u32[]{:S(2)}, u32[]{:S(2)}) collective-permute-start(f32[2,1,1,256,128]{4,3,2,0,1:T(8,128)} %get-tuple-element.125), channel_id=1, source_target_pairs={{0,1},{1,2},{2,3},{4,5},{5,6},{6,7},{8,9},{9,10},{10,11},{12,13},{... | collective-permute-start | bytes 786440 | tf_op jit(solution)/shard_map/ppermute | solution.py:19
  (29 other events, 597.4 us)
where the time goes:
time: 570 us; the launch traced here: 568 us
  blocking collectives  363 us (64%)
  starting transfers between devices  80.8 us (14%)
  other arithmetic  43.5 us (8%)
  matrix products  40.9 us (7%)
  local copies, waits for them, and re-layouts  32 us (6%)
  waiting for transfers between devices  5.72 us (1%)
    psum x5, blocking collectives, assemble(): arranged = lax.psum(canvas, ('gx', 'gy', 'gz'))  200 us
    psum x4, blocking collectives, totals(): return lax.psum(stacked, ('gx', 'gy', 'gz'))  163 us
    ppermute x15, starting transfers between devices, padded_2(): lax.ppermute(tail, axis, [(i, (i + 1) % count) for i in range(ends)])  61.4 us
    dot_general x5, matrix products, operate(): jnp.einsum('sij,sjr->sir', matrices, face_loads, preferred_element_type=j...  37.9 us
    ppermute x15, starting transfers between devices, padded_2(): lax.ppermute(head, axis, [((i + 1) % count, i) for i in range(ends)])  19.4 us
    reduce_sum x5, other arithmetic, coarse_source(): jnp.sum(upper_part - lower_part, axis=(3, 4))  12.7 us
  transfers between devices with their start and end apart: 30, of which 2 were waited for; matrix products, arithmetic and copies ran while one was open for 2% of the time, Pallas kernels for 0%

commit v1 on v0

v1 whole, which is shorter than its diff:
```python
import functools
import math

import jax
import jax.numpy as jnp
from jax import lax
from jax.experimental import pallas as pl
from jax.experimental.pallas import tpu as pltpu
from jax.sharding import PartitionSpec as P

ITERS = 4
MESH = pl.DeviceIdType.MESH
AXES = ("gx", "gy", "gz")
HIGHEST = lax.Precision.HIGHEST


def shifted(values, dimension, toward):
    length = values.shape[dimension]
    widths = [(0, 0)] * values.ndim
    if toward > 0:
        widths[dimension] = (0, 1)
        return lax.slice_in_dim(jnp.pad(values, widths), 1, length + 1, axis=dimension)
    widths[dimension] = (1, 0)
    return lax.slice_in_dim(jnp.pad(values, widths), 0, length, axis=dimension)


def coupling(glue, floating_flag):
    grid_shape = floating_flag.shape
    active = []
    for dimension in range(3):
        coordinate = lax.broadcasted_iota(jnp.int32, grid_shape, dimension)
        inside = (coordinate < grid_shape[dimension] - 1).astype(jnp.int32)
        active.append(inside * glue[..., dimension])
    return (jnp.stack(active, axis=-1), floating_flag)


def coarse_matrix(active, floating):
    grid_shape = floating.shape
    total_count = grid_shape[0] * grid_shape[1] * grid_shape[2]
    strides = (grid_shape[1] * grid_shape[2], grid_shape[2], 1)
    support = 2.0 / float(grid_shape[0] * grid_shape[0])
    degree = jnp.zeros(grid_shape, jnp.int32)
    for dimension in range(3):
        degree = degree + active[..., dimension] + shifted(active[..., dimension], dimension, -1)
    flat_float = floating.reshape(total_count).astype(jnp.float32)
    diagonal = jnp.where(
        flat_float > 0, degree.reshape(total_count).astype(jnp.float32) + support, 1.0
    )
    row_index = lax.broadcasted_iota(jnp.int32, (total_count, total_count), 0)
    col_index = lax.broadcasted_iota(jnp.int32, (total_count, total_count), 1)
    matrix = jnp.where(row_index == col_index, diagonal[:, None], 0.0)
    for dimension in range(3):
        link_weight = (
            (active[..., dimension] * floating * shifted(floating, dimension, 1))
            .reshape(total_count)
            .astype(jnp.float32)
        )
        lower = jnp.where(row_index == col_index + strides[dimension], link_weight[None, :], 0.0)
        upper = jnp.where(col_index == row_index + strides[dimension], link_weight[:, None], 0.0)
        matrix = matrix - upper - lower
    return matrix


def dot32(left, right):
    return jnp.dot(left, right, precision=HIGHEST, preferred_element_type=jnp.float32)


def column_sums(values):
    return jnp.sum(values, axis=0, keepdims=True)


def kernel(
    counts,
    block_x,
    face,
    flex_hbm,
    dual_hbm,
    coarse_ref,
    mask_ref,
    matrix_ref,
    mult_ref,
    out_ref,
    flex,
    dual,
    inverse,
    projector,
    load,
    trace,
    other,
    search,
    resid,
    applied,
    source,
    gathered,
    flex_sem,
    dual_sem,
    send_sem,
    recv_sem,
    gsend_sem,
    grecv_sem,
):
    nx, ny, nz = counts
    me = [lax.axis_index(axis) for axis in AXES]
    order = (2, 3, 4, 5, 0, 1)
    cases = coarse_ref.shape[1]
    total = coarse_ref.shape[0]
    grid_x = nx * block_x
    mode = 1.0 / math.sqrt(face)
    support = 2.0 / float(grid_x * grid_x)
    block_rows = -(-(block_x + 3) // 8) * 8
    devices = nx * ny * nz

    def peer(axis, step):
        return lax.rem(me[axis] + step, counts[axis])

    def flex_copy(i, f):
        rows = pl.ds(f * face, face)
        return pltpu.make_async_copy(
            flex_hbm.at[i, rows], flex.at[i, rows], flex_sem.at[i * 6 + f]
        )

    dual_copy = pltpu.make_async_copy(dual_hbm, dual, dual_sem)
    for f in order:
        for i in range(block_x):
            flex_copy(i, f).start()
        if f == 2:
            dual_copy.start()

    other[...] = jnp.zeros_like(other)
    barrier = pltpu.get_barrier_semaphore()
    for axis in range(3):
        for step in range(1, counts[axis]):
            pl.semaphore_signal(
                barrier, inc=1, device_id={AXES[axis]: peer(axis, step)}, device_id_type=MESH
            )

    inverse[...] = matrix_ref[...]
    lane = lax.broadcasted_iota(jnp.int32, (total, total), 1)
    line = lax.broadcasted_iota(jnp.int32, (total, total), 0)
    lane_one = lax.broadcasted_iota(jnp.int32, (1, total), 1)

    def eliminate(k, carry):
        values = inverse[...]
        pivot_row = inverse[pl.ds(k, 1), :]
        pivot = jnp.sum(jnp.where(lane_one == k, pivot_row, 0.0), axis=1, keepdims=True)
        column = jnp.sum(jnp.where(lane == k, values, 0.0), axis=1, keepdims=True)
        scale = 1.0 / pivot
        scaled = jnp.where(lane_one == k, scale, pivot_row * scale)
        rest = jnp.where(lane == k, 0.0, values) - column * scaled
        inverse[...] = jnp.where(line == k, scaled, rest)
        return carry

    lax.fori_loop(0, total, eliminate, 0)

    faces = 6 * block_x
    row = lax.broadcasted_iota(jnp.int32, (faces, total), 0)
    col = lax.broadcasted_iota(jnp.int32, (faces, total), 1)
    own = jnp.zeros((faces, total), jnp.int32)
    near = jnp.zeros((faces, total), jnp.int32)
    strides = (ny * nz, nz, 1)
    for i in range(block_x):
        here = ((me[0] * block_x + i) * ny + me[1]) * nz + me[2]
        for f in range(6):
            there = here + (strides[f // 2] if f % 2 else -strides[f // 2])
            own = jnp.where(row == i * 6 + f, here, own)
            near = jnp.where(row == i * 6 + f, there, near)
    difference = jnp.where(col == own, mode, 0.0) - jnp.where(col == near, mode, 0.0)
    difference = difference * mask_ref[0:faces, 0:1]
    projector[...] = dot32(difference, inverse[...])

    begin = dot32(projector[...], coarse_ref[...])
    resid[...] = jnp.zeros_like(resid)
    mult_ref[...] = jnp.zeros_like(mult_ref)
    source[...] = jnp.zeros_like(source)
    for i in range(block_x):
        for f in range(6):
            values = jnp.broadcast_to(begin[i * 6 + f : i * 6 + f + 1], (face, cases))
            search[i, f] = values
            load[i, f * face : (f + 1) * face] = values.astype(jnp.bfloat16)

    pl.semaphore_wait(barrier, sum(counts) - 3)

    def remote(i, f):
        if f >= 2:
            return True
        return i == 0 if f == 0 else i == block_x - 1

    def has_near(f):
        return me[f // 2] < counts[f // 2] - 1 if f % 2 else me[f // 2] > 0

    def face_copy(i, f):
        axis = f // 2
        target = me[axis] + (1 if f % 2 else -1)
        into = i
        if axis == 0:
            into = 0 if f % 2 else block_x - 1
        return pltpu.make_async_remote_copy(
            src_ref=trace.at[i, f],
            dst_ref=other.at[into, f ^ 1],
            send_sem=send_sem.at[i * 6 + f],
            recv_sem=recv_sem.at[into * 6 + (f ^ 1)],
            device_id={AXES[axis]: target},
            device_id_type=MESH,
        )

    def arrival(i, f):
        axis = f // 2
        return pltpu.make_async_remote_copy(
            src_ref=trace.at[i, f],
            dst_ref=other.at[i, f],
            send_sem=send_sem.at[i * 6 + f],
            recv_sem=recv_sem.at[i * 6 + f],
            device_id={AXES[axis]: me[axis] + (1 if f % 2 else -1)},
            device_id_type=MESH,
        )

    spans = (devices, ny * nz, nz, 1)
    place = (me[0] * ny + me[1]) * nz + me[2]

    def gather(slot):
        for axis in (2, 1, 0):
            width = spans[axis + 1]
            start = lax.div(place, width) * width
            rows = pl.ds(pl.multiple_of(start * block_rows, 8), width * block_rows)
            copies = []
            for step in range(1, counts[axis]):
                copy = pltpu.make_async_remote_copy(
                    src_ref=gathered.at[slot, rows],
                    dst_ref=gathered.at[slot, rows],
                    send_sem=gsend_sem.at[slot, axis, step],
                    recv_sem=grecv_sem.at[slot, axis, step],
                    device_id={AXES[axis]: peer(axis, step)},
                    device_id_type=MESH,
                )
                copy.start()
                copies.append(copy)
            for copy in copies:
                copy.wait()

    def iterate(it, carry):
        current, squared = carry
        slot = lax.rem(it, 2)
        first = it == 0
        last = it == ITERS

        for f in order:
            for i in range(block_x):

                @pl.when(first)
                def _():
                    flex_copy(i, f).wait()

                trace[i, f] = jnp.dot(
                    flex[i, f * face : (f + 1) * face, :],
                    load[i],
                    preferred_element_type=jnp.float32,
                )
                if f % 2:

                    @pl.when(first)
                    def _():
                        if f == 3 and i == 0:
                            dual_copy.wait()
                        trace[i, f] = trace[i, f] - dual[i, f // 2]

                if remote(i, f):

                    @pl.when(has_near(f))
                    def _():
                        face_copy(i, f).start()

        sums = [jnp.zeros((1, cases), jnp.float32) for _ in range(3)]
        sources = [jnp.zeros((1, cases), jnp.float32) for _ in range(block_x)]
        for f in (0, 1, 2, 3, 4, 5):
            for i in range(block_x):
                if remote(i, f):

                    @pl.when(has_near(f))
                    def _():
                        arrival(i, f).wait_recv()

                    partner = other[i, f]
                else:
                    partner = trace[i + (1 if f % 2 else -1), f ^ 1]
                row_of = i * 6 + f
                values = mask_ref[row_of : row_of + 1, :] * (trace[i, f] - partner)
                applied[i, f] = values
                sources[i] = sources[i] + column_sums(values)
                if f % 2:
                    sums[0] = sums[0] + column_sums(search[i, f] * values)
                    sums[1] = sums[1] + column_sums(resid[i, f] * values)
                    sums[2] = sums[2] + column_sums(values * values)
        sources = [
            sources[i] * mask_ref[faces + i : faces + i + 1, :] for i in range(block_x)
        ]
        lines = sources + sums
        lines = lines + [jnp.zeros((1, cases), jnp.float32)] * (block_rows - len(lines))
        gathered[slot, pl.ds(pl.multiple_of(place * block_rows, 8), block_rows)] = (
            jnp.concatenate(lines, axis=0)
        )
        gather(slot)

        totals = [
            column_sums(gathered[slot, pl.ds(block_x + j, devices, stride=block_rows), :])
            for j in range(3)
        ]
        step = jnp.where(first, 1.0, current / totals[0])
        plane = ny * nz
        for gx in range(nx):
            for i in range(block_x):
                at = (gx * block_x + i) * plane
                source[at : at + plane] = (
                    source[at : at + plane]
                    - step
                    * gathered[slot, pl.ds(gx * plane * block_rows + i, plane, stride=block_rows), :]
                )
        amplitude = dot32(inverse[...], source[...])
        spread = dot32(projector[...], source[...])
        squared = squared - 2.0 * step * totals[1] + step * step * totals[2]
        removed = column_sums(source[...] * amplitude)
        removed = removed + support * column_sums(amplitude * amplitude)
        renewed = squared - removed
        ratio = jnp.where(jnp.logical_or(first, last), 0.0, renewed / current)

        for i in range(block_x):
            for f in range(6):
                row_of = i * 6 + f
                old = search[i, f]
                left = resid[i, f] - step * applied[i, f]
                resid[i, f] = left
                fresh = (left - spread[row_of : row_of + 1]) + ratio * old
                search[i, f] = fresh
                load[i, f * face : (f + 1) * face] = fresh.astype(jnp.bfloat16)
                if f % 2:
                    mult_ref[i, f // 2] = mult_ref[i, f // 2] + step * old
                if remote(i, f):

                    @pl.when(has_near(f))
                    def _():
                        face_copy(i, f).wait_send()

        return renewed, squared

    zero = jnp.zeros((1, cases), jnp.float32)
    lax.fori_loop(0, ITERS + 1, iterate, (zero, zero))
    for i in range(block_x):
        for d in range(3):
            out_ref[i, d] = search[i, 2 * d + 1]


def per_device(counts, flexibility, dual_load, coarse_load, glue, floating_flag):
    block_x, block_y, block_z = dual_load.shape[:3]
    face, cases = dual_load.shape[4:]
    assert block_y == 1 and block_z == 1
    grid_x, grid_y, grid_z = floating_flag.shape
    total = grid_x * grid_y * grid_z
    nx, ny, nz = counts
    start = (lax.axis_index("gx") * block_x, lax.axis_index("gy"), lax.axis_index("gz"))
    active_int, floating_int = coupling(glue, floating_flag)
    matrix = coarse_matrix(active_int, floating_int)
    floating = floating_int.astype(jnp.float32)
    columns = []
    for d in range(3):
        columns.append(shifted(active_int[..., d], d, -1).astype(jnp.float32))
        columns.append(active_int[..., d].astype(jnp.float32))
    columns.append(floating / math.sqrt(face))
    table = lax.dynamic_slice(
        jnp.stack(columns, axis=-1), start + (0,), (block_x, 1, 1, 7)
    ).reshape(block_x, 7)
    masks = jnp.concatenate([table[:, :6].reshape(block_x * 6), table[:, 6]])
    rows = -(-(block_x * 7) // 8) * 8
    masks = jnp.pad(masks, (0, rows - block_x * 7))
    masks = jnp.broadcast_to(masks[:, None], (rows, cases))
    coarse = (floating[..., None] * coarse_load).reshape(total, cases)
    block_rows = -(-(block_x + 3) // 8) * 8
    devices = nx * ny * nz
    fields = (block_x, 6, face, cases)
    vmem = pl.BlockSpec(memory_space=pltpu.VMEM)
    hbm = pl.BlockSpec(memory_space=pl.ANY)
    out = jax.ShapeDtypeStruct((block_x, 3, face, cases), jnp.float32)
    most = max(counts)
    mult, resid = pl.pallas_call(
        functools.partial(kernel, counts, block_x, face),
        out_shape=(out, out),
        in_specs=[hbm, hbm, vmem, vmem, vmem],
        out_specs=(vmem, vmem),
        scratch_shapes=[
            pltpu.VMEM((block_x, 6 * face, 6 * face), jnp.bfloat16),
            pltpu.VMEM((block_x, 3, face, cases), jnp.float32),
            pltpu.VMEM((total, total), jnp.float32),
            pltpu.VMEM((6 * block_x, total), jnp.float32),
            pltpu.VMEM((block_x, 6 * face, cases), jnp.bfloat16),
            pltpu.VMEM(fields, jnp.float32),
            pltpu.VMEM(fields, jnp.float32),
            pltpu.VMEM(fields, jnp.float32),
            pltpu.VMEM(fields, jnp.float32),
            pltpu.VMEM(fields, jnp.float32),
            pltpu.VMEM((total, cases), jnp.float32),
            pltpu.VMEM((2, devices * block_rows, cases), jnp.float32),
            pltpu.SemaphoreType.DMA((6 * block_x,)),
            pltpu.SemaphoreType.DMA,
            pltpu.SemaphoreType.DMA((6 * block_x,)),
            pltpu.SemaphoreType.DMA((6 * block_x,)),
            pltpu.SemaphoreType.DMA((2, 3, most)),
            pltpu.SemaphoreType.DMA((2, 3, most)),
        ],
        compiler_params=pltpu.CompilerParams(collective_id=0, has_side_effects=True),
        name="feti_cg",
    )(
        flexibility.reshape(block_x, 6 * face, 6 * face),
        dual_load.reshape(block_x, 3, face, cases),
        coarse,
        masks,
        matrix,
    )
    shape = dual_load.shape
    return mult.reshape(shape), resid.reshape(shape)


def solution(mesh):
    counts = tuple(mesh.shape[axis] for axis in AXES)
    return jax.shard_map(
        functools.partial(per_device, counts),
        mesh=mesh,
        in_specs=(
            P("gx", "gy", "gz", None, None),
            P("gx", "gy", "gz", None, None, None),
            P(),
            P(),
            P(),
        ),
        out_specs=(P("gx", "gy", "gz", None, None, None), P("gx", "gy", "gz", None, None, None)),
        check_vma=False,
    )
```

time: 570 us -> 143 us (0.25)
  blocking collectives: 363 us -> 0 us
  Pallas kernels: 0 us -> 129 us
  starting transfers between devices: 80.8 us -> 0 us
  matrix products: 40.9 us -> 0 us
  other arithmetic: 43.5 us -> 7.11 us
  local copies, waits for them, and re-layouts: 32 us -> 5.62 us
  waiting for transfers between devices: 5.72 us -> 0 us
    psum x9 -> x0, blocking collectives: 363 us -> none  [the longest x5 200 us: assemble(): arranged = lax.psum(canvas, ('gx', 'gy', 'gz'))]
    pallas_call x0 -> x1, Pallas kernels: none -> 129 us  [per_device(): pl.pallas_call(functools.partial(kernel, counts, block_x, face), out_shap...]
    ppermute x30 -> x0, starting transfers between devices: 80.8 us -> none  [the longest x15 61.4 us: padded_2(): lax.ppermute(tail, axis, [(i, (i + 1) % count) for i in range(ends)])]
    dot_general x5 -> x0, matrix products: 37.9 us -> none  [operate(): jnp.einsum('sij,sjr->sir', matrices, face_loads, preferred_element_type=j...]
    another operation x30 -> x1, other arithmetic: 18.1 us -> 0.71 us  [per_device(): jnp.stack(columns, axis=-1)]
    reduce_sum x13 -> x0, other arithmetic: 15.7 us -> none  [the longest x5 12.7 us: coarse_source(): jnp.sum(upper_part - lower_part, axis=(3, 4))]
    slice x24 -> x1, local copies, waits for them, and re-layouts: 11.9 us -> 0.18 us  [per_device(): masks = jnp.concatenate([table[:, :6].reshape(block_x * 6), table[:, 6]])]
    dot_general x5 -> x0, local copies, waits for them, and re-layouts: 10 us -> none  [operate(): jnp.einsum('sij,sjr->sir', matrices, face_loads, preferred_element_type=j...]
  transfers between devices with their start and end apart: 30 -> 0, of which waited for: 2 -> 0; matrix products, arithmetic and copies ran while one was open for 2% -> 0% of each run, Pallas kernels for 0% -> 0%
where the time goes in v1:
time: 143 us; the launch traced here: 142 us
  Pallas kernels  129 us (90%)
  other arithmetic  7.11 us (5%)
  local copies, waits for them, and re-layouts  5.62 us (4%)
    pallas_call x1, Pallas kernels, per_device(): pl.pallas_call(functools.partial(kernel, counts, block_x, face), out_shap...  129 us
    unnamed x2, local copies, waits for them, and re-layouts  4.13 us

profile of v1, /device:TPU:0, one launch (start us, length us, event | category | flops | bytes accessed | tf_op | source)
XLA Modules:
  0.0 142.0 jit_solution(716698650460517003)
XLA Ops:
  0.7 1.0 multiply_convert_fusion
  1.6 0.1 convert_element_type.98
  1.7 0.1 convert_element_type.94
  1.8 0.1 convert_element_type.96
  1.9 0.8 add_select_fusion
  2.7 0.1 select_n.47
  2.8 0.8 select_subtract_fusion.matrix_ref
  3.6 1.5 %broadcast_multiply_fusion = f32[4,4,4,128]{3,2,1,0:T(4,128)} fusion(f32[4,4,4,128]{3,2,1,0:T(4,128)} %param.7, f32[4,4,4]{2,1,0:T(4,128)S(1)} %get-tuple-element.20), kind=kLoop, calls=%fused_computation.17 | loop fusion | flops 8192 | bytes 65792 | tf_op jit(solution)/shard_map/mul | solution.py:374
  5.0 0.8 constant_dynamic-update-slice_fusion.5
  5.8 0.8 constant_dynamic-update-slice_fusion.3
  6.6 0.1 constant_dynamic-update-slice_fusion.2
  6.7 0.7 constant_dynamic-update-slice_fusion.1
  7.4 0.7 constant_dynamic-update-slice_fusion
  8.1 0.1 constant_dynamic-slice_fusion
  8.2 0.1 copy.16
  8.3 0.1 reshape.90
  8.3 0.2 slice_reduce_fusion
  8.5 0.1 fusion.7
  8.6 0.7 broadcast_in_dim.70.mask_ref
  9.3 128.6 %feti_cg.1 = (f32[2,3,256,128]{3,2,1,0:T(8,128)}, f32[2,3,256,128]{3,2,1,0:T(8,128)}) custom-call(bf16[2,1536,1536]{2,1,0:T(8,128)(2,1)} %bitcast.49, f32[2,3,256,128]{3,2,1,0:T(8,128)} %bitcast.50, f32[64,128]{1,0:T(8,128)} %bitcast.53, f32[16,128]{1,0:T(8,128)} %broadcast_in_dim.70.mask_ref, f32[64,64]{1,0:T(8,128)} %select_subtract_fusion.matrix_ref), custom_call_target="tpu_custom_call" | custom-call | tf_op jit(solution)/shard_map/feti_cg/pallas_call | solution.py:382
  137.9 2.1 %copy.30 = f32[2,1,1,3,256,128]{5,4,3,2,1,0:T(8,128)} copy(f32[2,1,1,3,256,128]{5,4,3,2,1,0:T(8,128)} %bitcast.52) | data formatting | bytes 1572864
  139.9 2.1 %copy.31 = f32[2,1,1,3,256,128]{5,4,3,2,1,0:T(8,128)} copy(f32[2,1,1,3,256,128]{5,4,3,2,1,0:T(8,128)} %bitcast.51) | data formatting | bytes 1572864
  (5 shorter events, 0.0 us)

commit v2 on v1

v2 whole, which is shorter than its diff:
```python
import functools
import math

import jax
import jax.numpy as jnp
from jax import lax
from jax.experimental import pallas as pl
from jax.experimental.pallas import tpu as pltpu
from jax.sharding import PartitionSpec as P

ITERS = 4
MESH = pl.DeviceIdType.MESH
AXES = ("gx", "gy", "gz")
HIGHEST = lax.Precision.HIGHEST


def dot32(left, right):
    return jnp.dot(left, right, precision=HIGHEST, preferred_element_type=jnp.float32)


def column_sums(values):
    return jnp.sum(values, axis=0, keepdims=True)


def kernel(
    counts,
    block_x,
    face,
    flex_hbm,
    dual_hbm,
    coarse_ref,
    pack_ref,
    mult_ref,
    out_ref,
    begin_ref,
    spread_ref,
    flex,
    dual,
    inverse,
    projector,
    masks,
    load,
    trace,
    other,
    fresh,
    search,
    resid,
    applied,
    source,
    applied_source,
    gathered,
    face_sums,
    near_sums,
    flex_sem,
    dual_sem,
    send_sem,
    recv_sem,
    ssend_sem,
    srecv_sem,
    gsend_sem,
    grecv_sem,
):
    nx, ny, nz = counts
    me = [lax.axis_index(axis) for axis in AXES]
    cases = coarse_ref.shape[1]
    total = coarse_ref.shape[0]
    grid = (nx * block_x, ny, nz)
    mode = 1.0 / math.sqrt(face)
    support = 2.0 / float(grid[0] * grid[0])
    block_rows = -(-(block_x + 4) // 8) * 8
    devices = nx * ny * nz
    faces = 6 * block_x
    strides = (ny * nz, nz, 1)

    def peer(axis, step):
        return lax.rem(me[axis] + step, counts[axis])

    def flex_copy(i, f):
        rows = pl.ds(f * face, face)
        return pltpu.make_async_copy(
            flex_hbm.at[i, rows], flex.at[i, rows], flex_sem.at[i * 6 + f]
        )

    dual_copy = pltpu.make_async_copy(dual_hbm, dual, dual_sem)
    for f in (2, 3, 4, 5, 0, 1):
        for i in range(block_x):
            flex_copy(i, f).start()
        if f == 2:
            dual_copy.start()

    other[...] = jnp.zeros_like(other)
    near_sums[...] = jnp.zeros_like(near_sums)
    barrier = pltpu.get_barrier_semaphore()
    for axis in range(3):
        for step in range(1, counts[axis]):
            pl.semaphore_signal(
                barrier, inc=1, device_id={AXES[axis]: peer(axis, step)}, device_id_type=MESH
            )

    lane = lax.broadcasted_iota(jnp.int32, (total, total), 1)
    line = lax.broadcasted_iota(jnp.int32, (total, total), 0)
    lane_one = lax.broadcasted_iota(jnp.int32, (1, total), 1)
    tall = lax.broadcasted_iota(jnp.int32, (total, cases), 0)
    floating = pack_ref[3 * total : 4 * total, :]

    def pick(choice, values):
        return jnp.dot(choice, values, preferred_element_type=jnp.float32)

    degree = jnp.zeros((total, cases), jnp.float32)
    bands = jnp.zeros((total, total), jnp.float32)
    for d in range(3):
        place_d = lax.rem(lax.div(tall, strides[d]), grid[d])
        active = jnp.where(place_d < grid[d] - 1, pack_ref[d * total : (d + 1) * total, :], 0.0)
        above = jnp.where(lane == line + strides[d], 1.0, 0.0)
        below = jnp.where(lane == line - strides[d], 1.0, 0.0)
        active_below = pick(below, active)
        degree = degree + active + active_below
        link_above = active * floating * pick(above, floating)
        link_below = active_below * floating * pick(below, floating)
        bands = bands + above * link_above[:, 0:1] + below * link_below[:, 0:1]
    diagonal = jnp.where(floating > 0.0, degree + support, 1.0)
    inverse[...] = jnp.where(lane == line, diagonal[:, 0:1], 0.0) - bands

    def eliminate(k, carry):
        values = inverse[...]
        pivot_row = inverse[pl.ds(k, 1), :]
        pivot = jnp.sum(jnp.where(lane_one == k, pivot_row, 0.0), axis=1, keepdims=True)
        column = jnp.sum(jnp.where(lane == k, values, 0.0), axis=1, keepdims=True)
        scale = 1.0 / pivot
        scaled = jnp.where(lane_one == k, scale, pivot_row * scale)
        rest = jnp.where(lane == k, 0.0, values) - column * scaled
        inverse[...] = jnp.where(line == k, scaled, rest)
        return carry

    lax.fori_loop(0, total, eliminate, 0)

    mask_rows = masks.shape[0]
    wide = lax.broadcasted_iota(jnp.int32, (mask_rows, 4 * total), 0)
    across = lax.broadcasted_iota(jnp.int32, (mask_rows, 4 * total), 1)
    row = lax.broadcasted_iota(jnp.int32, (faces, total), 0)
    col = lax.broadcasted_iota(jnp.int32, (faces, total), 1)
    own = jnp.zeros((faces, total), jnp.int32)
    near = jnp.zeros((faces, total), jnp.int32)
    chosen = jnp.full((mask_rows, 4 * total), -1, jnp.int32)
    for i in range(block_x):
        spot = (me[0] * block_x + i, me[1], me[2])
        here = (spot[0] * ny + spot[1]) * nz + spot[2]
        for f in range(6):
            d = f // 2
            there = here + (strides[d] if f % 2 else -strides[d])
            own = jnp.where(row == i * 6 + f, here, own)
            near = jnp.where(row == i * 6 + f, there, near)
            if f % 2:
                entry = jnp.where(spot[d] < grid[d] - 1, d * total + here, -1)
            else:
                entry = jnp.where(spot[d] > 0, d * total + there, -1)
            chosen = jnp.where(wide == i * 6 + f, entry, chosen)
        chosen = jnp.where(wide == faces + i, 3 * total + here, chosen)
    masks[...] = pick(jnp.where(across == chosen, 1.0, 0.0), pack_ref[...])
    difference = jnp.where(col == own, mode, 0.0) - jnp.where(col == near, mode, 0.0)
    difference = difference * masks[0:faces, 0:1]
    projector[...] = dot32(difference, inverse[...])

    begin = dot32(projector[...], floating * coarse_ref[...])
    search[...] = jnp.zeros_like(search)
    applied[...] = jnp.zeros_like(applied)
    resid[...] = jnp.zeros_like(resid)
    mult_ref[...] = jnp.zeros_like(mult_ref)
    source[...] = jnp.zeros_like(source)
    applied_source[...] = jnp.zeros_like(applied_source)
    face_sums[...] = jnp.zeros_like(face_sums)
    for i in range(block_x):
        for f in range(6):
            line_f = begin[i * 6 + f : i * 6 + f + 1]
            values = jnp.broadcast_to(line_f, (face, cases))
            fresh[i, f] = values
            load[i, f * face : (f + 1) * face] = values.astype(jnp.bfloat16)
            if f % 2:
                begin_ref[i, f // 2] = line_f

    pl.semaphore_wait(barrier, sum(counts) - 3)

    def remote(i, f):
        if f >= 2:
            return True
        return i == 0 if f == 0 else i == block_x - 1

    def has_near(f):
        return me[f // 2] < counts[f // 2] - 1 if f % 2 else me[f // 2] > 0

    def neighbour(f):
        return {AXES[f // 2]: me[f // 2] + (1 if f % 2 else -1)}

    def face_copy(slot, i, f, into):
        return pltpu.make_async_remote_copy(
            src_ref=trace.at[i, f],
            dst_ref=other.at[slot, into, f ^ 1],
            send_sem=send_sem.at[i * 6 + f],
            recv_sem=recv_sem.at[slot, into * 6 + (f ^ 1)],
            device_id=neighbour(f),
            device_id_type=MESH,
        )

    def send_face(slot, i, f):
        into = i
        if f < 2:
            into = 0 if f % 2 else block_x - 1
        return face_copy(slot, i, f, into)

    def arrival(slot, i, f):
        return pltpu.make_async_remote_copy(
            src_ref=trace.at[i, f],
            dst_ref=other.at[slot, i, f],
            send_sem=send_sem.at[i * 6 + f],
            recv_sem=recv_sem.at[slot, i * 6 + f],
            device_id=neighbour(f),
            device_id_type=MESH,
        )

    def sum_copy(f, g):
        return pltpu.make_async_remote_copy(
            src_ref=face_sums.at[f],
            dst_ref=near_sums.at[g],
            send_sem=ssend_sem.at[f],
            recv_sem=srecv_sem.at[g],
            device_id=neighbour(f),
            device_id_type=MESH,
        )

    spans = (devices, ny * nz, nz, 1)
    place = (me[0] * ny + me[1]) * nz + me[2]

    def gather(slot):
        for axis in (2, 1, 0):
            width = spans[axis + 1]
            start = lax.div(place, width) * width
            rows = pl.ds(pl.multiple_of(start * block_rows, 8), width * block_rows)
            copies = []
            for step in range(1, counts[axis]):
                copy = pltpu.make_async_remote_copy(
                    src_ref=gathered.at[slot, rows],
                    dst_ref=gathered.at[slot, rows],
                    send_sem=gsend_sem.at[slot, axis, step],
                    recv_sem=grecv_sem.at[slot, axis, step],
                    device_id={AXES[axis]: peer(axis, step)},
                    device_id_type=MESH,
                )
                copy.start()
                copies.append(copy)
            for copy in copies:
                copy.wait()

    def iterate(it, carry):
        before, curve = carry
        slot = lax.rem(it, 2)
        first = it == 0

        ww = jnp.zeros((1, cases), jnp.float32)
        wq = jnp.zeros((1, cases), jnp.float32)
        wt = jnp.zeros((1, cases), jnp.float32)
        pt = jnp.zeros((1, cases), jnp.float32)
        for d in (1, 2, 0):
            for f in (2 * d, 2 * d + 1):
                for i in range(block_x):

                    @pl.when(first)
                    def _():
                        flex_copy(i, f).wait()

                    trace[i, f] = jnp.dot(
                        flex[i, f * face : (f + 1) * face, :],
                        load[i],
                        preferred_element_type=jnp.float32,
                    )
                    if f % 2:

                        @pl.when(first)
                        def _():
                            if f == 3 and i == 0:
                                dual_copy.wait()
                            trace[i, f] = trace[i, f] - dual[i, f // 2]

                    face_sums[f, i : i + 1] = column_sums(trace[i, f])

                @pl.when(has_near(f))
                def _():
                    sum_copy(f, f ^ 1).start()
                    for i in range(block_x):
                        if remote(i, f):
                            send_face(slot, i, f).start()

        for f in range(6):
            for i in range(block_x):
                values = trace[i, f]
                now = fresh[i, f]
                wt = wt + column_sums(now * values)
                pt = pt + column_sums(search[i, f] * values)
                if f % 2:
                    ww = ww + column_sums(now * now)
                    wq = wq + column_sums(now * applied[i, f])

        sources = [jnp.zeros((1, cases), jnp.float32) for _ in range(block_x)]
        for f in (2, 3, 4, 5, 0, 1):

            @pl.when(has_near(f))
            def _():
                sum_copy(f, f).wait_recv()

            for i in range(block_x):
                step = 1 if f % 2 else -1
                if f >= 2:
                    partner = near_sums[f, i : i + 1]
                elif remote(i, f):
                    k = block_x - 1 - i
                    partner = near_sums[f, k : k + 1]
                else:
                    partner = face_sums[f ^ 1, i + step : i + step + 1]
                row_of = i * 6 + f
                sources[i] = sources[i] + masks[row_of : row_of + 1, :] * (
                    face_sums[f, i : i + 1] - partner
                )
        lines = [
            sources[i] * (mode * masks[faces + i : faces + i + 1, :]) for i in range(block_x)
        ]
        lines = lines + [ww, wt, wq, pt]
        lines = lines + [jnp.zeros((1, cases), jnp.float32)] * (block_rows - len(lines))
        gathered[slot, pl.ds(pl.multiple_of(place * block_rows, 8), block_rows)] = (
            jnp.concatenate(lines, axis=0)
        )
        gather(slot)

        ww, wt, wq, pt = [
            column_sums(gathered[slot, pl.ds(block_x + j, devices, stride=block_rows), :])
            for j in range(4)
        ]
        ratio = jnp.where(it <= 1, 0.0, ww / before)
        curve = wt + ratio * (wq + pt) + ratio * ratio * curve
        length = jnp.where(first, 1.0, ww / curve)
        plane = ny * nz
        for gx in range(nx):
            for i in range(block_x):
                at = (gx * block_x + i) * plane
                part = (
                    gathered[slot, pl.ds(gx * plane * block_rows + i, plane, stride=block_rows), :]
                    + ratio * applied_source[at : at + plane]
                )
                applied_source[at : at + plane] = part
                source[at : at + plane] = source[at : at + plane] - length * part
        spread = dot32(projector[...], source[...])
        moved = jnp.where(first, 0.0, length)

        for f in (0, 1, 4, 5, 2, 3):
            for i in range(block_x):
                if remote(i, f):

                    @pl.when(has_near(f))
                    def _():
                        arrival(slot, i, f).wait_recv()
                        send_face(slot, i, f).wait_send()

                    partner = other[slot, i, f]
                else:
                    partner = trace[i + (1 if f % 2 else -1), f ^ 1]
                row_of = i * 6 + f
                jump = masks[row_of : row_of + 1, :] * (trace[i, f] - partner)
                product = jump + ratio * applied[i, f]
                applied[i, f] = product
                toward = fresh[i, f] + ratio * search[i, f]
                search[i, f] = toward
                if f % 2:
                    mult_ref[i, f // 2] = mult_ref[i, f // 2] + moved * toward
                left = resid[i, f] - length * product
                resid[i, f] = left
                renewed = left - spread[row_of : row_of + 1]
                fresh[i, f] = renewed
                load[i, f * face : (f + 1) * face] = renewed.astype(jnp.bfloat16)
                if f % 2:
                    spread_ref[i, f // 2] = spread[row_of : row_of + 1]

            @pl.when(has_near(f))
            def _():
                sum_copy(f, f ^ 1).wait_send()

        return ww, curve

    zero = jnp.zeros((1, cases), jnp.float32)
    lax.fori_loop(0, ITERS + 1, iterate, (zero, zero))
    for i in range(block_x):
        for d in range(3):
            out_ref[i, d] = resid[i, 2 * d + 1]


def per_device(counts, flexibility, dual_load, coarse_load, glue, floating_flag):
    block_x, block_y, block_z = dual_load.shape[:3]
    face, cases = dual_load.shape[4:]
    assert block_y == 1 and block_z == 1
    grid_x, grid_y, grid_z = floating_flag.shape
    total = grid_x * grid_y * grid_z
    nx, ny, nz = counts
    packed = jnp.concatenate([jnp.moveaxis(glue, 3, 0).reshape(3 * total), floating_flag.reshape(total)])
    packed = jnp.broadcast_to(packed.astype(jnp.float32)[:, None], (4 * total, cases))
    coarse = coarse_load.reshape(total, cases)
    block_rows = -(-(block_x + 4) // 8) * 8
    sum_rows = -(-block_x // 8) * 8
    mask_rows = -(-(block_x * 7) // 8) * 8
    devices = nx * ny * nz
    fields = (block_x, 6, face, cases)
    vmem = pl.BlockSpec(memory_space=pltpu.VMEM)
    hbm = pl.BlockSpec(memory_space=pl.ANY)
    out = jax.ShapeDtypeStruct((block_x, 3, face, cases), jnp.float32)
    most = max(counts)
    small = jax.ShapeDtypeStruct((block_x, 3, 1, cases), jnp.float32)
    mult, resid, begin, spread = pl.pallas_call(
        functools.partial(kernel, counts, block_x, face),
        out_shape=(out, out, small, small),
        in_specs=[hbm, hbm, vmem, vmem],
        out_specs=(vmem, vmem, vmem, vmem),
        scratch_shapes=[
            pltpu.VMEM((block_x, 6 * face, 6 * face), jnp.bfloat16),
            pltpu.VMEM((block_x, 3, face, cases), jnp.float32),
            pltpu.VMEM((total, total), jnp.float32),
            pltpu.VMEM((6 * block_x, total), jnp.float32),
            pltpu.VMEM((mask_rows, cases), jnp.float32),
            pltpu.VMEM((block_x, 6 * face, cases), jnp.bfloat16),
            pltpu.VMEM(fields, jnp.float32),
            pltpu.VMEM((2,) + fields, jnp.float32),
            pltpu.VMEM(fields, jnp.float32),
            pltpu.VMEM(fields, jnp.float32),
            pltpu.VMEM(fields, jnp.float32),
            pltpu.VMEM(fields, jnp.float32),
            pltpu.VMEM((total, cases), jnp.float32),
            pltpu.VMEM((total, cases), jnp.float32),
            pltpu.VMEM((2, devices * block_rows, cases), jnp.float32),
            pltpu.VMEM((6, sum_rows, cases), jnp.float32),
            pltpu.VMEM((6, sum_rows, cases), jnp.float32),
            pltpu.SemaphoreType.DMA((6 * block_x,)),
            pltpu.SemaphoreType.DMA,
            pltpu.SemaphoreType.DMA((6 * block_x,)),
            pltpu.SemaphoreType.DMA((2, 6 * block_x)),
            pltpu.SemaphoreType.DMA((6,)),
            pltpu.SemaphoreType.DMA((6,)),
            pltpu.SemaphoreType.DMA((2, 3, most)),
            pltpu.SemaphoreType.DMA((2, 3, most)),
        ],
        compiler_params=pltpu.CompilerParams(collective_id=0, has_side_effects=True),
        name="feti_cg",
    )(
        flexibility.reshape(block_x, 6 * face, 6 * face),
        dual_load.reshape(block_x, 3, face, cases),
        coarse,
        packed,
    )
    shape = dual_load.shape
    return (mult + begin).reshape(shape), (resid - spread).reshape(shape)


def solution(mesh):
    counts = tuple(mesh.shape[axis] for axis in AXES)
    return jax.shard_map(
        functools.partial(per_device, counts),
        mesh=mesh,
        in_specs=(
            P("gx", "gy", "gz", None, None),
            P("gx", "gy", "gz", None, None, None),
            P(),
            P(),
            P(),
        ),
        out_specs=(P("gx", "gy", "gz", None, None, None), P("gx", "gy", "gz", None, None, None)),
        check_vma=False,
    )
```

time: 143 us -> 113 us (0.79)
  Pallas kernels: 129 us -> 105 us
  other arithmetic: 7.11 us -> 2.72 us
  local copies, waits for them, and re-layouts: 5.62 us -> 3.76 us
    pallas_call x1, Pallas kernels: 129 us -> 105 us  [per_device(): pl.pallas_call(functools.partial(kernel, counts, block_x, face), out_shap...]
    unnamed x2 -> x0, local copies, waits for them, and re-layouts: 4.13 us -> none
    mul x1 -> x0, other arithmetic: 1.46 us -> none  [per_device(): coarse = (floating[..., None] * coarse_load).reshape(total, cases)]
where the time goes in v2:
time: 113 us
  Pallas kernels  105 us (93%)
  local copies, waits for them, and re-layouts  3.76 us (3%)
  other arithmetic  2.72 us (2%)
    pallas_call x1, Pallas kernels, per_device(): pl.pallas_call(functools.partial(kernel, counts, block_x, face), out_shap...  105 us
    unnamed x1, other arithmetic  2.64 us

profile of v2, /device:TPU:0, one launch (start us, length us, event | category | flops | bytes accessed | tf_op | source)
XLA Modules:
  0.0 112.5 jit_solution(5051073219652186962)
XLA Ops:
  0.6 0.8 concatenate.12
  1.4 0.7 copy.9
  2.2 0.1 concatenate.11
  2.3 0.1 add_convert_fusion
  2.4 0.8 broadcast_in_dim.2.pack_ref
  3.1 105.4 %feti_cg.1 = (f32[2,3,256,128]{3,2,1,0:T(8,128)}, f32[2,3,256,128]{3,2,1,0:T(8,128)}, f32[2,3,1,128]{3,2,1,0:T(1,128)}, f32[2,3,1,128]{3,2,1,0:T(1,128)}) custom-call(bf16[2,1536,1536]{2,1,0:T(8,128)(2,1)} %bitcast.18, f32[2,3,256,128]{3,2,1,0:T(8,128)} %bitcast.19, f32[64,128]{1,0:T(8,128)} %bitcast.20, f32[256,128]{1,0:T(8,128)} %broadcast_in_dim.2.pack_ref), custom_call_target="tpu_custom_call" | custom-call | tf_op jit(solution)/shard_map/feti_cg/pallas_call | solution.py:413
  108.5 0.7 copy.19
  109.2 0.7 copy.18
  109.9 2.6 %subtract_bitcast_fusion = (f32[2,1,1,3,256,128]{5,4,3,2,1,0:T(8,128)}, f32[2,1,1,3,256,128]{5,4,3,2,1,0:T(8,128)}) fusion(f32[2,3,256,128]{3,2,1,0:T(8,128)} %get-tuple-element.8, f32[2,3,128]{2,1,0:T(4,128)S(1)} %copy.13, f32[2,3,256,128]{3,2,1,0:T(8,128)} %get-tuple-element.6, f32[2,3,128]{2,1,0:T(4,128)S(1)} %copy.11), kind=kLoop, calls=%fused_computation | loop fusion | flops 393216 | bytes 3151872
  (2 shorter events, 0.0 us)

commit v3 on v2

--- a/solution.py
+++ b/solution.py
@@ -75,6 +75,18 @@
     def peer(axis, step):
         return lax.rem(me[axis] + step, counts[axis])
 
+    def plane_peers():
+        found = []
+        for step_y in range(ny):
+            for step_z in range(nz):
+                if step_y or step_z:
+                    target = {"gy": peer(1, step_y), "gz": peer(2, step_z)}
+                    found.append((step_y * nz + step_z, target))
+        return found
+
+    def line_peers():
+        return [(step, {"gx": peer(0, step)}) for step in range(1, nx)]
+
     def flex_copy(i, f):
         rows = pl.ds(f * face, face)
         return pltpu.make_async_copy(
@@ -91,11 +103,8 @@
     other[...] = jnp.zeros_like(other)
     near_sums[...] = jnp.zeros_like(near_sums)
     barrier = pltpu.get_barrier_semaphore()
-    for axis in range(3):
-        for step in range(1, counts[axis]):
-            pl.semaphore_signal(
-                barrier, inc=1, device_id={AXES[axis]: peer(axis, step)}, device_id_type=MESH
-            )
+    for target in plane_peers() + line_peers():
+        pl.semaphore_signal(barrier, inc=1, device_id=target[1], device_id_type=MESH)
 
     lane = lax.broadcasted_iota(jnp.int32, (total, total), 1)
     line = lax.broadcasted_iota(jnp.int32, (total, total), 0)
@@ -178,7 +187,7 @@
             if f % 2:
                 begin_ref[i, f // 2] = line_f
 
-    pl.semaphore_wait(barrier, sum(counts) - 3)
+    pl.semaphore_wait(barrier, ny * nz + nx - 2)
 
     def remote(i, f):
         if f >= 2:
@@ -227,28 +236,25 @@
             device_id_type=MESH,
         )
 
-    spans = (devices, ny * nz, nz, 1)
+    plane = ny * nz
     place = (me[0] * ny + me[1]) * nz + me[2]
-
-    def gather(slot):
-        for axis in (2, 1, 0):
-            width = spans[axis + 1]
-            start = lax.div(place, width) * width
-            rows = pl.ds(pl.multiple_of(start * block_rows, 8), width * block_rows)
-            copies = []
-            for step in range(1, counts[axis]):
-                copy = pltpu.make_async_remote_copy(
-                    src_ref=gathered.at[slot, rows],
-                    dst_ref=gathered.at[slot, rows],
-                    send_sem=gsend_sem.at[slot, axis, step],
-                    recv_sem=grecv_sem.at[slot, axis, step],
-                    device_id={AXES[axis]: peer(axis, step)},
-                    device_id_type=MESH,
-                )
-                copy.start()
-                copies.append(copy)
-            for copy in copies:
-                copy.wait()
+    own_rows = pl.ds(pl.multiple_of(place * block_rows, 8), block_rows)
+    plane_rows = pl.ds(pl.multiple_of(me[0] * plane * block_rows, 8), plane * block_rows)
+
+    def spread_out(slot, rows, peers, first):
+        copies = []
+        for number, target in peers:
+            copy = pltpu.make_async_remote_copy(
+                src_ref=gathered.at[slot, rows],
+                dst_ref=gathered.at[slot, rows],
+                send_sem=gsend_sem.at[slot, first + number],
+                recv_sem=grecv_sem.at[slot, first + number],
+                device_id=target,
+                device_id_type=MESH,
+            )
+            copy.start()
+            copies.append(copy)
+        return copies
 
     def iterate(it, carry):
         before, curve = carry
@@ -286,7 +292,7 @@
                 def _():
                     sum_copy(f, f ^ 1).start()
                     for i in range(block_x):
-                        if remote(i, f):
+                        if f < 2 and remote(i, f) or f >= 2 and i == 0:
                             send_face(slot, i, f).start()
 
         for f in range(6):
@@ -324,10 +330,20 @@
         ]
         lines = lines + [ww, wt, wq, pt]
         lines = lines + [jnp.zeros((1, cases), jnp.float32)] * (block_rows - len(lines))
-        gathered[slot, pl.ds(pl.multiple_of(place * block_rows, 8), block_rows)] = (
-            jnp.concatenate(lines, axis=0)
-        )
-        gather(slot)
+        gathered[slot, own_rows] = jnp.concatenate(lines, axis=0)
+        copies = spread_out(slot, own_rows, plane_peers(), 0)
+        for f in (2, 3, 4, 5):
+
+            @pl.when(has_near(f))
+            def _():
+                for i in range(1, block_x):
+                    send_face(slot, i, f).start()
+
+        for copy in copies:
+            copy.wait_recv()
+        lines_out = spread_out(slot, plane_rows, line_peers(), plane)
+        for copy in lines_out:
+            copy.wait_recv()
 
         ww, wt, wq, pt = [
             column_sums(gathered[slot, pl.ds(block_x + j, devices, stride=block_rows), :])
@@ -336,7 +352,6 @@
         ratio = jnp.where(it <= 1, 0.0, ww / before)
         curve = wt + ratio * (wq + pt) + ratio * ratio * curve
         length = jnp.where(first, 1.0, ww / curve)
-        plane = ny * nz
         for gx in range(nx):
             for i in range(block_x):
                 at = (gx * block_x + i) * plane
@@ -349,8 +364,8 @@
         spread = dot32(projector[...], source[...])
         moved = jnp.where(first, 0.0, length)
 
-        for f in (0, 1, 4, 5, 2, 3):
-            for i in range(block_x):
+        for i in range(block_x):
+            for f in (0, 1, 4, 5, 2, 3):
                 if remote(i, f):
 
                     @pl.when(has_near(f))
@@ -377,10 +392,14 @@
                 if f % 2:
                     spread_ref[i, f // 2] = spread[row_of : row_of + 1]
 
+        for f in range(6):
+
             @pl.when(has_near(f))
             def _():
                 sum_copy(f, f ^ 1).wait_send()
 
+        for copy in copies + lines_out:
+            copy.wait_send()
         return ww, curve
 
     zero = jnp.zeros((1, cases), jnp.float32)
@@ -408,7 +427,6 @@
     vmem = pl.BlockSpec(memory_space=pltpu.VMEM)
     hbm = pl.BlockSpec(memory_space=pl.ANY)
     out = jax.ShapeDtypeStruct((block_x, 3, face, cases), jnp.float32)
-    most = max(counts)
     small = jax.ShapeDtypeStruct((block_x, 3, 1, cases), jnp.float32)
     mult, resid, begin, spread = pl.pallas_call(
         functools.partial(kernel, counts, block_x, face),
@@ -439,8 +457,8 @@
             pltpu.SemaphoreType.DMA((2, 6 * block_x)),
             pltpu.SemaphoreType.DMA((6,)),
             pltpu.SemaphoreType.DMA((6,)),
-            pltpu.SemaphoreType.DMA((2, 3, most)),
-            pltpu.SemaphoreType.DMA((2, 3, most)),
+            pltpu.SemaphoreType.DMA((2, ny * nz + nx)),
+            pltpu.SemaphoreType.DMA((2, ny * nz + nx)),
         ],
         compiler_params=pltpu.CompilerParams(collective_id=0, has_side_effects=True),
         name="feti_cg",

time: 113 us -> 92 us (0.81)
  Pallas kernels: 105 us -> 83.8 us
    pallas_call x1, Pallas kernels: 105 us -> 83.8 us  [per_device(): pl.pallas_call(functools.partial(kernel, counts, block_x, face), out_shap...]
where the time goes in v3:
time: 92 us; the launch traced here: 90.9 us
  Pallas kernels  83.8 us (91%)
  local copies, waits for them, and re-layouts  3.76 us (4%)
  other arithmetic  2.72 us (3%)
    pallas_call x1, Pallas kernels, per_device(): pl.pallas_call(functools.partial(kernel, counts, block_x, face), out_shap...  83.8 us
    unnamed x1, other arithmetic  2.64 us

profile of v3, /device:TPU:0, one launch (start us, length us, event | category | flops | bytes accessed | tf_op | source)
XLA Modules:
  0.0 90.9 jit_solution(1935694744841100605)
XLA Ops:
  0.6 0.8 concatenate.12
  1.4 0.7 copy.9
  2.2 0.1 concatenate.11
  2.3 0.1 add_convert_fusion
  2.4 0.8 broadcast_in_dim.2.pack_ref
  3.1 83.8 %feti_cg.1 = (f32[2,3,256,128]{3,2,1,0:T(8,128)}, f32[2,3,256,128]{3,2,1,0:T(8,128)}, f32[2,3,1,128]{3,2,1,0:T(1,128)}, f32[2,3,1,128]{3,2,1,0:T(1,128)}) custom-call(bf16[2,1536,1536]{2,1,0:T(8,128)(2,1)} %bitcast.18, f32[2,3,256,128]{3,2,1,0:T(8,128)} %bitcast.19, f32[64,128]{1,0:T(8,128)} %bitcast.20, f32[256,128]{1,0:T(8,128)} %broadcast_in_dim.2.pack_ref), custom_call_target="tpu_custom_call" | custom-call | tf_op jit(solution)/shard_map/feti_cg/pallas_call | solution.py:431
  86.9 0.7 copy.19
  87.6 0.7 copy.18
  88.3 2.6 %subtract_bitcast_fusion = (f32[2,1,1,3,256,128]{5,4,3,2,1,0:T(8,128)}, f32[2,1,1,3,256,128]{5,4,3,2,1,0:T(8,128)}) fusion(f32[2,3,256,128]{3,2,1,0:T(8,128)} %get-tuple-element.8, f32[2,3,128]{2,1,0:T(4,128)S(1)} %copy.13, f32[2,3,256,128]{3,2,1,0:T(8,128)} %get-tuple-element.6, f32[2,3,128]{2,1,0:T(4,128)S(1)} %copy.11), kind=kLoop, calls=%fused_computation | loop fusion | flops 393216 | bytes 3151872
  (2 shorter events, 0.0 us)

commit v4 on v3

--- a/solution.py
+++ b/solution.py
@@ -141,7 +141,36 @@
         inverse[...] = jnp.where(line == k, scaled, rest)
         return carry
 
-    lax.fori_loop(0, total, eliminate, 0)
+    def eliminate_pair(half, carry):
+        k = 2 * half
+        values = inverse[...]
+        rows = [inverse[pl.ds(k + j, 1), :] for j in range(2)]
+        (a, b), (c, d) = [
+            [
+                jnp.sum(jnp.where(lane_one == k + j, pivot, 0.0), axis=1, keepdims=True)
+                for j in range(2)
+            ]
+            for pivot in rows
+        ]
+        scale = 1.0 / (a * d - b * c)
+        block = ((d * scale, -b * scale), (-c * scale, a * scale))
+        rest = jnp.where(jnp.logical_or(lane == k, lane == k + 1), 0.0, values)
+        results = []
+        for j in range(2):
+            column = jnp.sum(jnp.where(lane == k + j, values, 0.0), axis=1, keepdims=True)
+            left, right = block[j]
+            scaled = left * rows[0] + right * rows[1]
+            scaled = jnp.where(lane_one == k, left, jnp.where(lane_one == k + 1, right, scaled))
+            rest = rest - column * scaled
+            results.append(scaled)
+        rest = jnp.where(line == k, results[0], rest)
+        inverse[...] = jnp.where(line == k + 1, results[1], rest)
+        return carry
+
+    if total % 2:
+        lax.fori_loop(0, total, eliminate, 0)
+    else:
+        lax.fori_loop(0, total // 2, eliminate_pair, 0)
 
     mask_rows = masks.shape[0]
     wide = lax.broadcasted_iota(jnp.int32, (mask_rows, 4 * total), 0)

time: 92 us -> 89.3 us (0.971)
  Pallas kernels: 83.8 us -> 81.1 us
    pallas_call x1, Pallas kernels: 83.8 us -> 81.1 us  [per_device(): pl.pallas_call(functools.partial(kernel, counts, block_x, face), out_shap...]
where the time goes in v4:
time: 89.3 us; the launch traced here: 88.3 us
  Pallas kernels  81.1 us (91%)
  local copies, waits for them, and re-layouts  3.76 us (4%)
  other arithmetic  2.72 us (3%)
    pallas_call x1, Pallas kernels, per_device(): pl.pallas_call(functools.partial(kernel, counts, block_x, face), out_shap...  81.1 us
    unnamed x1, other arithmetic  2.64 us

profile of v4, /device:TPU:0, one launch (start us, length us, event | category | flops | bytes accessed | tf_op | source)
XLA Modules:
  0.0 88.3 jit_solution(7970688979724572566)
XLA Ops:
  0.6 0.8 concatenate.12
  1.4 0.7 copy.9
  2.2 0.1 concatenate.11
  2.3 0.1 add_convert_fusion
  2.4 0.8 broadcast_in_dim.2.pack_ref
  3.1 81.1 %feti_cg.1 = (f32[2,3,256,128]{3,2,1,0:T(8,128)}, f32[2,3,256,128]{3,2,1,0:T(8,128)}, f32[2,3,1,128]{3,2,1,0:T(1,128)}, f32[2,3,1,128]{3,2,1,0:T(1,128)}) custom-call(bf16[2,1536,1536]{2,1,0:T(8,128)(2,1)} %bitcast.18, f32[2,3,256,128]{3,2,1,0:T(8,128)} %bitcast.19, f32[64,128]{1,0:T(8,128)} %bitcast.20, f32[256,128]{1,0:T(8,128)} %broadcast_in_dim.2.pack_ref), custom_call_target="tpu_custom_call" | custom-call | tf_op jit(solution)/shard_map/feti_cg/pallas_call | solution.py:460
  84.3 0.7 copy.19
  84.9 0.7 copy.18
  85.6 2.6 %subtract_bitcast_fusion = (f32[2,1,1,3,256,128]{5,4,3,2,1,0:T(8,128)}, f32[2,1,1,3,256,128]{5,4,3,2,1,0:T(8,128)}) fusion(f32[2,3,256,128]{3,2,1,0:T(8,128)} %get-tuple-element.8, f32[2,3,128]{2,1,0:T(4,128)S(1)} %copy.13, f32[2,3,256,128]{3,2,1,0:T(8,128)} %get-tuple-element.6, f32[2,3,128]{2,1,0:T(4,128)S(1)} %copy.11), kind=kLoop, calls=%fused_computation | loop fusion | flops 393216 | bytes 3151872
  (2 shorter events, 0.0 us)
